TPU v7x, 512 devices: a whole 4x8x8 slice. The times are simulated.
512 devices in a mesh: rep: 4 (over z_lo), fsdp: 16 (over y, core), tp: 8 (over z_hi, x).
Axes of the slice: x: 4, y: 8, z: 8 (z_hi: 2, z_lo: 4; z = z_hi * 4 + z_lo), core: 2. Of those that a mesh axis runs over, the one named last changes fastest.
Arguments:
- delta_attn: float32 [4, 4, 768, 768], P('rep', None, 'fsdp', 'tp'), may hold values from -4 to 4
- delta_in: float32 [4, 768, 3072], P('rep', 'fsdp', 'tp'), may hold values from -4 to 4
- delta_out: float32 [4, 3072, 768], P('rep', 'fsdp', 'tp'), may hold values from -4 to 4
- delta_small: float32 [4, 1920], P('rep'), may hold values from -4 to 4
- emb_left: float32 [4, 8, 4016, 64], P('rep', 'tp', 'fsdp'), may hold values from -6 to 6
- emb_right: float32 [4, 64, 768], P('rep'), may hold values from -0.75 to 0.75
- anchor_attn: float32 [8, 294912], P('tp', 'fsdp'), may hold values from -6 to 6
- anchor_in: float32 [8, 294912], P('tp', 'fsdp'), may hold values from -6 to 6
- anchor_out: float32 [8, 294912], P('tp', 'fsdp'), may hold values from -6 to 6
- anchor_small: float32 [1920], P('fsdp'), may hold values from -6 to 6
- anchor_emb: float32 [8, 16, 4, 48192], P('tp', 'fsdp', 'rep'), may hold values from -6 to 6
- moment_attn: float32 [8, 294912], P('tp', 'fsdp'), may hold values from -4 to 4
- moment_in: float32 [8, 294912], P('tp', 'fsdp'), may hold values from -4 to 4
- moment_out: float32 [8, 294912], P('tp', 'fsdp'), may hold values from -4 to 4
- moment_small: float32 [1920], P('fsdp'), may hold values from -4 to 4
- moment_emb: float32 [8, 16, 4, 48192], P('tp', 'fsdp', 'rep'), may hold values from -4 to 4
Outputs:
- new_attn: float32 [4, 768, 768], P(None, 'fsdp', 'tp')
- new_in: float32 [768, 3072], P('fsdp', 'tp')
- new_out: float32 [3072, 768], P('fsdp', 'tp')
- new_small: float32 [1920], replicated
- new_emb: float32 [32128, 768], P('tp', 'fsdp')
- next_attn: float32 [8, 294912], P('tp', 'fsdp')
- next_in: float32 [8, 294912], P('tp', 'fsdp')
- next_out: float32 [8, 294912], P('tp', 'fsdp')
- next_small: float32 [1920], P('fsdp')
- next_emb: float32 [8, 16, 4, 48192], P('tp', 'fsdp', 'rep')
All inputs are finite; a program needn't handle non-finite values.
Results may differ from a plain program's by a relative error of at most 0.000071.
Values sent between devices are 32-bit elements; how exact they have to be, the bound alone decides.
A program may use at most 64 MiB of HBM per device.

v0:
```python
import jax
import jax.numpy as jnp
from jax import lax
from jax.sharding import PartitionSpec as P

OUTER_RATE = 0.7
MOMENTUM_COEF = 0.9


def nesterov(anchor, moment, mean_delta):
    moment_next = MOMENTUM_COEF * moment + mean_delta
    updated = anchor - OUTER_RATE * (mean_delta + MOMENTUM_COEF * moment_next)
    return (updated, moment_next)


def to_blocks(matrix, lead, shards):
    local_rows = matrix.shape[-2]
    width = matrix.shape[-1] // shards
    shaped = matrix.reshape(lead, local_rows, shards, width)
    return jnp.transpose(shaped, (2, 3, 0, 1))


def from_blocks(blocks):
    shards, width, lead, local_rows = blocks.shape
    return jnp.transpose(blocks, (2, 3, 0, 1)).reshape(lead, local_rows, shards * width)


def on_device(
    delta_attn,
    delta_in,
    delta_out,
    delta_small,
    emb_left,
    emb_right,
    anchor_attn,
    anchor_in,
    anchor_out,
    anchor_small,
    anchor_emb,
    moment_attn,
    moment_in,
    moment_out,
    moment_small,
    moment_emb,
):
    groups = lax.axis_size("rep")
    shards = lax.axis_size("fsdp")
    send_attn = to_blocks(delta_attn[0], 4, shards)
    send_in = to_blocks(delta_in[0][None], 1, shards)
    send_out = to_blocks(delta_out[0][None], 1, shards)
    flat_attn, flat_in, flat_out = (
        lax.all_to_all(send_attn, "fsdp", split_axis=0, concat_axis=3, tiled=True),
        lax.all_to_all(send_in, "fsdp", split_axis=0, concat_axis=3, tiled=True),
        lax.all_to_all(send_out, "fsdp", split_axis=0, concat_axis=3, tiled=True),
    )
    block_shapes = (flat_attn.shape, flat_in.shape, flat_out.shape)
    portion = anchor_small.shape[0]
    small_local = lax.dynamic_slice_in_dim(
        delta_small[0], lax.axis_index("fsdp") * portion, portion, 0
    )[None, :]
    differences = (
        flat_attn.reshape(flat_attn.shape[1] * flat_attn.shape[2], flat_attn.shape[3]),
        flat_in.reshape(flat_in.shape[1], flat_in.shape[3]),
        flat_out.reshape(flat_out.shape[1], flat_out.shape[3]),
        small_local,
    )
    anchors = (
        anchor_attn.reshape(differences[0].shape),
        anchor_in.reshape(differences[1].shape),
        anchor_out.reshape(differences[2].shape),
        anchor_small[None, :],
    )
    moments = (
        moment_attn.reshape(differences[0].shape),
        moment_in.reshape(differences[1].shape),
        moment_out.reshape(differences[2].shape),
        moment_small[None, :],
    )
    totals = lax.psum((differences[0], differences[1], differences[2], differences[3]), "rep")
    updated_list = []
    moment_list = []
    for summed, anchor_part, moment_part in zip(totals, anchors, moments):
        updated, moment_next = nesterov(anchor_part, moment_part, summed / groups)
        updated_list.append(updated)
        moment_list.append(moment_next)
    back_attn = updated_list[0].reshape(block_shapes[0])
    back_in = updated_list[1].reshape(block_shapes[1])
    back_out = updated_list[2].reshape(block_shapes[2])
    train_attn, train_in, train_out = (
        lax.all_to_all(back_attn, "fsdp", split_axis=3, concat_axis=0, tiled=True),
        lax.all_to_all(back_in, "fsdp", split_axis=3, concat_axis=0, tiled=True),
        lax.all_to_all(back_out, "fsdp", split_axis=3, concat_axis=0, tiled=True),
    )
    new_attn = from_blocks(train_attn)
    new_in = from_blocks(train_in)[0]
    new_out = from_blocks(train_out)[0]
    new_small = lax.all_gather(updated_list[3].reshape(portion), "fsdp", axis=0, tiled=True)
    left_local = emb_left[0, 0]
    right_local = emb_right[0]
    block_rows = left_local.shape[0]
    column_count = right_local.shape[1] // groups
    product_term = jnp.dot(
        left_local, right_local, precision=lax.Precision.HIGHEST, preferred_element_type=jnp.float32
    )
    summed_emb = lax.psum_scatter(product_term, "rep", scatter_dimension=1, tiled=True)
    anchor_rows = anchor_emb[0, 0, 0].reshape(block_rows, column_count)
    moment_rows = moment_emb[0, 0, 0].reshape(block_rows, column_count)
    new_emb_part, next_emb_part = nesterov(anchor_rows, moment_rows, summed_emb / groups)
    full_rows = lax.all_gather(new_emb_part, "rep", axis=1, tiled=True)
    new_emb = lax.all_to_all(full_rows, "fsdp", split_axis=1, concat_axis=0, tiled=True)
    return (
        new_attn,
        new_in,
        new_out,
        new_small,
        new_emb,
        moment_list[0].reshape(moment_attn.shape),
        moment_list[1].reshape(moment_in.shape),
        moment_list[2].reshape(moment_out.shape),
        moment_list[3].reshape(moment_small.shape),
        next_emb_part.reshape(moment_emb.shape),
    )


def solution(mesh):
    placed = (
        P("rep", None, "fsdp", "tp"),
        P("rep", "fsdp", "tp"),
        P("rep", "fsdp", "tp"),
        P("rep", None),
        P("rep", "tp", "fsdp", None),
        P("rep", None, None),
        P("tp", "fsdp"),
        P("tp", "fsdp"),
        P("tp", "fsdp"),
        P("fsdp"),
        P("tp", "fsdp", "rep", None),
        P("tp", "fsdp"),
        P("tp", "fsdp"),
        P("tp", "fsdp"),
        P("fsdp"),
        P("tp", "fsdp", "rep", None),
    )
    return jax.shard_map(
        on_device,
        mesh=mesh,
        in_specs=placed,
        out_specs=(
            P(None, "fsdp", "tp"),
            P("fsdp", "tp"),
            P("fsdp", "tp"),
            P(),
            P("tp", "fsdp"),
            P("tp", "fsdp"),
            P("tp", "fsdp"),
            P("tp", "fsdp"),
            P("fsdp"),
            P("tp", "fsdp", "rep", None),
        ),
        check_vma=False,
    )
```

profile of v0, /device:TPU:32, one launch (start us, length us, event | category | flops | bytes accessed | tf_op | source)
XLA Modules:
  0.0 245.8 jit_solution(11660199578842059813)
XLA Ops:
  7.2 1.1 copy.88
  8.2 0.8 reshape.155
  9.1 8.8 %all-to-all-start.2 = ((f32[16,1,1152]{2,1,0:T(1,128)}), f32[16,1,1152]{2,1,0:T(1,128)S(1)}, u32[]{:S(2)}, u32[]{:S(2)}) async-start(f32[16,1,1152]{2,1,0:T(1,128)} %reshape.155), calls=%async_computation.2 | async-start | bytes 147456 | tf_op jit(solution)/shard_map/all_to_all | solution.py:53
  17.9 1.0 copy.83
  18.9 0.9 reshape.151
  19.8 1.4 all-to-all-done.2
  21.2 8.2 %all-to-all-start = ((f32[16,1,1152]{2,1,0:T(1,128)}), f32[16,1,1152]{2,1,0:T(1,128)S(1)}, u32[]{:S(2)}, u32[]{:S(2)}) async-start(f32[16,1,1152]{2,1,0:T(1,128)} %reshape.151), calls=%async_computation | async-start | bytes 147456 | tf_op jit(solution)/shard_map/all_to_all | solution.py:52
  29.3 1.6 copy.94
  31.0 0.6 broadcast.90
  31.5 0.8 reduce.28
  32.6 8.2 %all-to-all-start.4 = ((f32[16,6,1,192]{3,2,1,0:T(1,128)}), f32[16,6,1,192]{3,2,1,0:T(1,128)S(1)}, u32[]{:S(2)}, u32[]{:S(2)}) async-start(f32[16,6,1,192]{3,2,1,0:T(1,128)} %bitcast.21), calls=%async_computation.4 | async-start | bytes 196608 | tf_op jit(solution)/shard_map/all_to_all | solution.py:54
  40.9 0.8 reshape.93
  41.6 0.8 reduce.27
  42.7 0.8 reshape.89
  43.5 1.1 all-to-all-done.4
  44.6 0.7 reshape.96
  45.6 1.7 fusion
  47.9 0.8 reduce.26
  49.2 0.8 reduce.25
  50.1 0.6 reshape.92
  50.7 0.6 mul.77
  51.4 0.8 reduce.24
  52.2 0.6 reshape.88
  53.1 0.6 mul.73
  54.4 0.6 multiply_reduce_fusion
  55.1 0.8 copy.99
  55.9 48.3 %all-reduce.4.cloned.1.call-done = (f32[24,768]{1,0:T(8,128)}, f32[24,768]{1,0:T(8,128)}, f32[6,3072]{1,0:T(8,128)}) async-done(((f32[24,768]{1,0:T(8,128)}, f32[24,768]{1,0:T(8,128)}, f32[6,3072]{1,0:T(8,128)}), (f32[24,768]{1,0:T(8,128)}, f32[24,768]{1,0:T(8,128)}, f32[6,3072]{1,0:T(8,128)})) %all-reduce.4.cloned.1.call-update) | async-done | bytes 221200 | tf_op jit(solution)/shard_map/psum | solution.py:79
  104.1 1.6 fusion.2
  105.7 1.6 copy.96
  107.3 13.7 %reduce.32 = f32[3072,6]{1,0:T(8,128)S(1)} reduce(f32[3072,1,1,6]{3,2,1,0:T(1,128)S(1)} %bitcast.106, f32[]{:T(128)} %broadcast.90), dimensions={1,2}, to_apply=%bitcast.99.reduce_sub_computation | reduce | bytes 147460
  121.1 1.9 reshape.159
  123.0 7.2 %all-to-all-start.5 = ((f32[16,1,1152]{2,1,0:T(1,128)}), f32[16,1,1152]{2,1,0:T(1,128)S(1)}, u32[]{:S(2)}, u32[]{:S(2)}) async-start(f32[16,1,1152]{2,1,0:T(1,128)} %reshape.159), calls=%async_computation.5 | async-start | bytes 147456 | tf_op jit(solution)/shard_map/all_to_all | solution.py:92
  130.2 0.7 fusion.5
  131.2 1.6 reduce.30
  132.8 0.9 reshape.157
  133.7 0.7 fusion.4
  134.4 0.7 copy.85
  135.1 2.5 %reshape.153 = f32[16,1,1152]{2,1,0:T(1,128)} reshape(f32[768,1,4,6]{3,2,1,0:T(4,128)S(1)} %bitcast.103) | data formatting | bytes 147456
  137.6 7.2 %all-to-all-start.3 = ((f32[16,1,1152]{2,1,0:T(1,128)}), f32[16,1,1152]{2,1,0:T(1,128)S(1)}, u32[]{:S(2)}, u32[]{:S(2)}) async-start(f32[16,1,1152]{2,1,0:T(1,128)} %reshape.157), calls=%async_computation.3 | async-start | bytes 147456 | tf_op jit(solution)/shard_map/all_to_all | solution.py:91
  144.9 1.0 multiply_add_fusion
  145.9 2.2 all-to-all-done.3
  148.1 8.1 %all-to-all-start.1 = ((f32[16,1,1152]{2,1,0:T(1,128)}), f32[16,1,1152]{2,1,0:T(1,128)S(1)}, u32[]{:S(2)}, u32[]{:S(2)}) async-start(f32[16,1,1152]{2,1,0:T(1,128)} %reshape.153), calls=%async_computation.1 | async-start | bytes 147456 | tf_op jit(solution)/shard_map/all_to_all | solution.py:90
  156.3 18.3 %all_gather.7 = f32[251,768]{0,1:T(8,128)} all-gather(f32[251,192]{0,1:T(8,128)S(1)} %get-tuple-element.54), channel_id=1, replica_groups=mesh['rep'=4,'fsdp'=16,'tp'=8] {'rep'}, dimensions={1}, use_global_device_ids=true | all-gather | bytes 963840 | tf_op jit(solution)/shard_map/all_gather | solution.py:109
  174.6 7.2 %all-to-all-start.6 = ((f32[251,16,48]{0,2,1:T(8,128)}), f32[251,16,48]{0,2,1:T(8,128)S(1)}, u32[]{:S(2)}, u32[]{:S(2)}) async-start(f32[251,16,48]{0,2,1:T(8,128)} %bitcast.35), calls=%async_computation.7 | async-start | bytes 1572864 | tf_op jit(solution)/shard_map/all_to_all | solution.py:110
  181.8 1.3 dynamic-slice.1
  183.7 0.8 constant_dynamic-slice_fusion
  184.5 10.2 %psum.31 = f32[1,120]{1,0:T(1,128)S(1)} all-reduce(f32[1,120]{1,0:T(1,128)S(1)} %constant_dynamic-slice_fusion), channel_id=1, replica_groups=mesh['rep'=4,'fsdp'=16,'tp'=8] {'rep'}, use_global_device_ids=true, to_apply=%region_3.0 | all-reduce | flops 120 | bytes 960 | tf_op jit(solution)/shard_map/psum | solution.py:79
  194.8 26.9 %all-reduce = f32[1920]{0:T(1024)} all-reduce(f32[1920]{0:T(1024)S(1)} %bitcast_dynamic-update-slice_fusion), channel_id=2, replica_groups=mesh['rep'=4,'fsdp'=16,'tp'=8] {'fsdp'}, use_global_device_ids=true, to_apply=%add | all-reduce | flops 1920 | bytes 15360 | tf_op jit(solution)/shard_map/all_gather | solution.py:97
  222.2 0.7 copy.111
  222.9 0.7 copy.110
  223.6 0.7 copy.109
  224.4 0.8 reduce.33
  225.2 2.5 reshape.160
  227.6 0.6 copy.108
  228.4 0.7 copy.105
  229.1 0.8 reduce.31
  229.9 0.7 reshape.158
  230.9 0.7 copy.104
  231.7 0.8 reduce.29
  232.5 2.0 reshape.154
  234.5 0.8 copy.106
  235.4 0.8 copy.103
  236.3 0.9 reshape.103
  237.7 1.3 all_to_all.110
  (84 shorter events, 4.9 us)
Async XLA Ops:
  7.2 38.4 %copy-start = (f32[1,64,768]{2,1,0:T(8,128)S(1)}, f32[1,64,768]{2,1,0:T(8,128)}, u32[]{:S(2)}) copy-start(f32[1,64,768]{2,1,0:T(8,128)} %param.21) | copy-start | bytes 589828
  9.1 12.1 %all-to-all-start.2 = ((f32[16,1,1152]{2,1,0:T(1,128)}), f32[16,1,1152]{2,1,0:T(1,128)S(1)}, u32[]{:S(2)}, u32[]{:S(2)}) async-start(f32[16,1,1152]{2,1,0:T(1,128)} %reshape.155), calls=%async_computation.2 | async-start | bytes 147456 | tf_op jit(solution)/shard_map/all_to_all | solution.py:53
  21.2 11.4 %all-to-all-start = ((f32[16,1,1152]{2,1,0:T(1,128)}), f32[16,1,1152]{2,1,0:T(1,128)S(1)}, u32[]{:S(2)}, u32[]{:S(2)}) async-start(f32[16,1,1152]{2,1,0:T(1,128)} %reshape.151), calls=%async_computation | async-start | bytes 147456 | tf_op jit(solution)/shard_map/all_to_all | solution.py:52
  32.3 13.3 %copy-start.21 = (f32[1,1,251,64]{2,3,1,0:T(8,128)S(1)}, f32[1,1,251,64]{2,3,1,0:T(8,128)}, u32[]{:S(2)}) copy-start(f32[1,1,251,64]{2,3,1,0:T(8,128)} %param.20) | copy-start | bytes 192772
  32.6 12.0 %all-to-all-start.4 = ((f32[16,6,1,192]{3,2,1,0:T(1,128)}), f32[16,6,1,192]{3,2,1,0:T(1,128)S(1)}, u32[]{:S(2)}, u32[]{:S(2)}) async-start(f32[16,6,1,192]{3,2,1,0:T(1,128)} %bitcast.21), calls=%async_computation.4 | async-start | bytes 196608 | tf_op jit(solution)/shard_map/all_to_all | solution.py:54
  40.8 63.4 %all-reduce.4.cloned.1.call-start = ((), (), s32[]{:S(2)}) async-start(), calls=%async_computation.9 | async-start | bytes 491520 | tf_op jit(solution)/shard_map/psum | solution.py:79
  42.7 5.2 %copy-start.13 = (f32[1,18432]{1,0:T(1,128)S(1)}, f32[1,18432]{1,0:T(1,128)}, u32[]{:S(2)}) copy-start(f32[1,18432]{1,0:T(1,128)} %param.24) | copy-start | bytes 221188
  42.7 6.0 %copy-start.17 = (f32[1,18432]{1,0:T(1,128)S(1)}, f32[1,18432]{1,0:T(1,128)}, u32[]{:S(2)}) copy-start(f32[1,18432]{1,0:T(1,128)} %param.29) | copy-start | bytes 221188
  42.7 6.0 %copy-start.18 = (f32[1,18432]{1,0:T(1,128)S(1)}, f32[1,18432]{1,0:T(1,128)}, u32[]{:S(2)}) copy-start(f32[1,18432]{1,0:T(1,128)} %param.28) | copy-start | bytes 221188
  44.6 4.7 %copy-start.14 = (f32[1,18432]{1,0:T(1,128)S(1)}, f32[1,18432]{1,0:T(1,128)}, u32[]{:S(2)}) copy-start(f32[1,18432]{1,0:T(1,128)} %param.23) | copy-start | bytes 221188
  45.3 6.0 %copy-start.15 = (f32[1,18432]{1,0:T(1,128)S(1)}, f32[1,18432]{1,0:T(1,128)}, u32[]{:S(2)}) copy-start(f32[1,18432]{1,0:T(1,128)} %param.22) | copy-start | bytes 221188
  45.4 7.5 %copy-start.16 = (f32[1,18432]{1,0:T(1,128)S(1)}, f32[1,18432]{1,0:T(1,128)}, u32[]{:S(2)}) copy-start(f32[1,18432]{1,0:T(1,128)} %param.27) | copy-start | bytes 221188
  45.4 8.3 %copy-start.11 = (f32[1,1,1,48192]{3,2,1,0:T(1,128)S(1)}, f32[1,1,1,48192]{3,2,1,0:T(1,128)}, u32[]{:S(2)}) copy-start(f32[1,1,1,48192]{3,2,1,0:T(1,128)} %param.26) | copy-start | bytes 578308
  45.4 99.5 %reduce-scatter.2.cloned.1.call-start = ((), (), s32[]{:S(2)}) async-start(), calls=%async_computation.8 | async-start | bytes 983040 | tf_op jit(solution)/shard_map/reduce_scatter | solution.py:105
  47.4 7.0 %copy-start.12 = (f32[1,1,1,48192]{3,2,1,0:T(1,128)S(1)}, f32[1,1,1,48192]{3,2,1,0:T(1,128)}, u32[]{:S(2)}) copy-start(f32[1,1,1,48192]{3,2,1,0:T(1,128)} %param.31) | copy-start | bytes 578308
  121.0 9.2 %copy-start.9 = (f32[24,768]{1,0:T(8,128)S(1)}, f32[24,768]{1,0:T(8,128)}, u32[]{:S(2)}) copy-start(f32[24,768]{1,0:T(8,128)} %reshape.92) | copy-start | bytes 221188
  121.0 9.2 %copy-start.10 = (f32[24,768]{1,0:T(8,128)S(1)}, f32[24,768]{1,0:T(8,128)}, u32[]{:S(2)}) copy-start(f32[24,768]{1,0:T(8,128)} %mul.77) | copy-start | bytes 221188
  121.0 9.2 %copy-start.20 = (f32[24,768]{1,0:T(8,128)S(1)}, f32[24,768]{1,0:T(8,128)}, u32[]{:S(2)}) copy-start(f32[24,768]{1,0:T(8,128)} %get-tuple-element.51) | copy-start | bytes 221188
  121.0 12.7 %copy-start.7 = (f32[24,768]{1,0:T(8,128)S(1)}, f32[24,768]{1,0:T(8,128)}, u32[]{:S(2)}) copy-start(f32[24,768]{1,0:T(8,128)} %reshape.88) | copy-start | bytes 221188
  121.0 12.7 %copy-start.8 = (f32[24,768]{1,0:T(8,128)S(1)}, f32[24,768]{1,0:T(8,128)}, u32[]{:S(2)}) copy-start(f32[24,768]{1,0:T(8,128)} %mul.73) | copy-start | bytes 221188
  121.0 12.7 %copy-start.19 = (f32[24,768]{1,0:T(8,128)S(1)}, f32[24,768]{1,0:T(8,128)}, u32[]{:S(2)}) copy-start(f32[24,768]{1,0:T(8,128)} %get-tuple-element.50) | copy-start | bytes 221188
  123.0 14.6 %all-to-all-start.5 = ((f32[16,1,1152]{2,1,0:T(1,128)}), f32[16,1,1152]{2,1,0:T(1,128)S(1)}, u32[]{:S(2)}, u32[]{:S(2)}) async-start(f32[16,1,1152]{2,1,0:T(1,128)} %reshape.159), calls=%async_computation.5 | async-start | bytes 147456 | tf_op jit(solution)/shard_map/all_to_all | solution.py:92
  134.4 10.5 %copy-start.1 = (f32[251,192]{0,1:T(8,128)S(1)}, f32[251,192]{0,1:T(8,128)}, u32[]{:S(2)}) copy-start(f32[251,192]{0,1:T(8,128)} %copy.99) | copy-start | bytes 578308
  137.6 10.5 %all-to-all-start.3 = ((f32[16,1,1152]{2,1,0:T(1,128)}), f32[16,1,1152]{2,1,0:T(1,128)S(1)}, u32[]{:S(2)}, u32[]{:S(2)}) async-start(f32[16,1,1152]{2,1,0:T(1,128)} %reshape.157), calls=%async_computation.3 | async-start | bytes 147456 | tf_op jit(solution)/shard_map/all_to_all | solution.py:91
  145.8 48.8 %copy-start.22 = (f32[120]{0:T(128)S(1)}, f32[120]{0:T(128)}, u32[]{:S(2)}) copy-start(f32[120]{0:T(128)} %param.25) | copy-start | bytes 1444
  145.9 48.8 %copy-start.23 = (f32[120]{0:T(128)S(1)}, f32[120]{0:T(128)}, u32[]{:S(2)}) copy-start(f32[120]{0:T(128)} %param.30) | copy-start | bytes 1444
  145.9 76.3 %copy-start.2 = (f32[1,1,6,3072]{3,2,1,0:T(8,128)S(1)}, f32[1,1,6,3072]{3,2,1,0:T(8,128)}, u32[]{:S(2)}) copy-start(f32[1,1,6,3072]{3,2,1,0:T(8,128)} %get-tuple-element.55) | copy-start | bytes 221188
  145.9 77.0 %copy-start.5 = (f32[1,1,24,768]{3,2,1,0:T(8,128)S(1)}, f32[1,1,24,768]{3,2,1,0:T(8,128)}, u32[]{:S(2)}) copy-start(f32[1,1,24,768]{3,2,1,0:T(8,128)} %get-tuple-element.57) | copy-start | bytes 221188
  145.9 77.7 %copy-start.6 = (f32[1,1,24,768]{3,2,1,0:T(8,128)S(1)}, f32[1,1,24,768]{3,2,1,0:T(8,128)}, u32[]{:S(2)}) copy-start(f32[1,1,24,768]{3,2,1,0:T(8,128)} %get-tuple-element.59) | copy-start | bytes 221188
  148.1 76.2 %copy-start.3 = (f32[16,1,1152]{2,1,0:T(1,128)}, f32[16,1,1152]{2,1,0:T(1,128)S(1)}, u32[]{:S(2)}) copy-start(f32[16,1,1152]{2,1,0:T(1,128)S(1)} %all-to-all-done.3) | copy-start | bytes 221188
  148.1 26.4 %all-to-all-start.1 = ((f32[16,1,1152]{2,1,0:T(1,128)}), f32[16,1,1152]{2,1,0:T(1,128)S(1)}, u32[]{:S(2)}, u32[]{:S(2)}) async-start(f32[16,1,1152]{2,1,0:T(1,128)} %reshape.153), calls=%async_computation.1 | async-start | bytes 147456 | tf_op jit(solution)/shard_map/all_to_all | solution.py:90
  174.6 62.6 %all-to-all-start.6 = ((f32[251,16,48]{0,2,1:T(8,128)}), f32[251,16,48]{0,2,1:T(8,128)S(1)}, u32[]{:S(2)}, u32[]{:S(2)}) async-start(f32[251,16,48]{0,2,1:T(8,128)} %bitcast.35), calls=%async_computation.7 | async-start | bytes 1572864 | tf_op jit(solution)/shard_map/all_to_all | solution.py:110
  227.6 1.5 copy-start.4
Sparse Core Ops, SparseCore 0:
  45.5 58.6 all-reduce.3
  107.8 30.1 reduce-scatter.1
where the time goes:
time: 247 us; the launch traced here: 246 us
  blocking collectives  55.4 us (22%)
  starting transfers between devices  55.2 us (22%)
  waiting for transfers between devices  53.1 us (21%)
  local copies, waits for them, and re-layouts  37.2 us (15%)
  other arithmetic  27.9 us (11%)
  between operations  15.3 us (6%)
    psum x1, waiting for transfers between devices, on_device(): lax.psum((differences[0], differences[1], differences[2], differences[3])...  48.3 us
    all_gather x1, blocking collectives, on_device(): lax.all_gather(updated_list[3].reshape(portion), 'fsdp', axis=0, tiled=True)  26.9 us
    unnamed x70, local copies, waits for them, and re-layouts  22.5 us
    unnamed x10, other arithmetic  21.2 us
    all_gather x1, blocking collectives, on_device(): full_rows = lax.all_gather(new_emb_part, 'rep', axis=1, tiled=True)  18.3 us
    psum x1, blocking collectives, on_device(): lax.psum((differences[0], differences[1], differences[2], differences[3])...  10.2 us
    all_to_all x1, starting transfers between devices, on_device(): lax.all_to_all(send_in, 'fsdp', split_axis=0, concat_axis=3, tiled=True)  8.82 us
    all_to_all x1, starting transfers between devices, on_device(): lax.all_to_all(send_out, 'fsdp', split_axis=0, concat_axis=3, tiled=True)  8.17 us
  transfers between devices with their start and end apart: 9, of which 5 were waited for; matrix products, arithmetic and copies ran while one was open for 25% of the time, Pallas kernels for 0%

commit v1 on v0

--- a/solution.py
+++ b/solution.py
@@ -94,7 +94,12 @@
     new_attn = from_blocks(train_attn)
     new_in = from_blocks(train_in)[0]
     new_out = from_blocks(train_out)[0]
-    new_small = lax.all_gather(updated_list[3].reshape(portion), "fsdp", axis=0, tiled=True)
+    new_small = jnp.concatenate(
+        lax.all_to_all(
+            jnp.stack([updated_list[3].reshape(portion)] * lax.axis_size("fsdp")), "fsdp", 0, 0
+        ),
+        axis=0,
+    )
     left_local = emb_left[0, 0]
     right_local = emb_right[0]
     block_rows = left_local.shape[0]

time: 247 us -> 217 us (0.88)
  the two profiles are of different devices: /device:TPU:32 before, /device:TPU:1 now
where the time goes in v1:
time: 217 us; the launch traced here: 216 us
  waiting for transfers between devices  59.1 us (27%)
  starting transfers between devices  48.3 us (22%)
  local copies, waits for them, and re-layouts  36 us (17%)
  other arithmetic  29 us (13%)
  blocking collectives  26.9 us (12%)
  between operations  14.6 us (7%)
    psum x1, waiting for transfers between devices, on_device(): lax.psum((differences[0], differences[1], differences[2], differences[3])...  24.9 us
    unnamed x9, other arithmetic  21.7 us
    unnamed x60, local copies, waits for them, and re-layouts  21.2 us
    all_gather x1, blocking collectives, on_device(): full_rows = lax.all_gather(new_emb_part, 'rep', axis=1, tiled=True)  16.2 us
    psum x1, blocking collectives, on_device(): lax.psum((differences[0], differences[1], differences[2], differences[3])...  10.7 us
    all_to_all x1, starting transfers between devices, on_device(): lax.all_to_all(send_in, 'fsdp', split_axis=0, concat_axis=3, tiled=True)  10.2 us
    all_to_all x1, starting transfers between devices, on_device(): lax.all_to_all(back_out, 'fsdp', split_axis=3, concat_axis=0, tiled=True)  9.62 us
    all_to_all x1, starting transfers between devices, on_device(): lax.all_to_all(full_rows, 'fsdp', split_axis=1, concat_axis=0, tiled=True)  9.32 us
  transfers between devices with their start and end apart: 10, of which 7 were waited for; matrix products, arithmetic and copies ran while one was open for 29% of the time, Pallas kernels for 0%

profile of v1, /device:TPU:1, one launch (start us, length us, event | category | flops | bytes accessed | tf_op | source)
XLA Modules:
  0.0 215.7 jit_solution(9350186677892509709)
XLA Ops:
  7.2 1.1 copy.88
  8.2 0.8 reshape.163
  9.1 10.2 %all-to-all-start.2 = ((f32[16,1,1152]{2,1,0:T(1,128)}), f32[16,1,1152]{2,1,0:T(1,128)S(1)}, u32[]{:S(2)}, u32[]{:S(2)}) async-start(f32[16,1,1152]{2,1,0:T(1,128)} %reshape.163), calls=%async_computation.2 | async-start | bytes 147456 | tf_op jit(solution)/shard_map/all_to_all | solution.py:53
  19.2 1.0 copy.83
  20.3 0.9 reshape.159
  21.1 6.1 %all-to-all-done.2 = f32[16,1,1152]{2,1,0:T(1,128)S(1)} async-done(((f32[16,1,1152]{2,1,0:T(1,128)}), f32[16,1,1152]{2,1,0:T(1,128)S(1)}, u32[]{:S(2)}, u32[]{:S(2)}) %all-to-all-start.2) | async-done | bytes 73760 | tf_op jit(solution)/shard_map/all_to_all | solution.py:53
  27.3 3.4 %all-to-all-start = ((f32[16,1,1152]{2,1,0:T(1,128)}), f32[16,1,1152]{2,1,0:T(1,128)S(1)}, u32[]{:S(2)}, u32[]{:S(2)}) async-start(f32[16,1,1152]{2,1,0:T(1,128)} %reshape.159), calls=%async_computation | async-start | bytes 147456 | tf_op jit(solution)/shard_map/all_to_all | solution.py:52
  30.7 1.6 copy.94
  32.9 0.8 reduce.32
  33.8 4.9 %all-to-all-done = f32[16,1,1152]{2,1,0:T(1,128)S(1)} async-done(((f32[16,1,1152]{2,1,0:T(1,128)}), f32[16,1,1152]{2,1,0:T(1,128)S(1)}, u32[]{:S(2)}, u32[]{:S(2)}) %all-to-all-start) | async-done | bytes 73760 | tf_op jit(solution)/shard_map/all_to_all | solution.py:52
  38.7 3.4 %all-to-all-start.4 = ((f32[16,6,1,192]{3,2,1,0:T(1,128)}), f32[16,6,1,192]{3,2,1,0:T(1,128)S(1)}, u32[]{:S(2)}, u32[]{:S(2)}) async-start(f32[16,6,1,192]{3,2,1,0:T(1,128)} %bitcast.21), calls=%async_computation.4 | async-start | bytes 196608 | tf_op jit(solution)/shard_map/all_to_all | solution.py:54
  42.2 0.8 reshape.101
  43.0 0.8 reduce.31
  44.1 0.8 reshape.97
  44.9 5.8 %all-to-all-done.4 = f32[16,6,1,192]{3,2,1,0:T(1,128)S(1)} async-done(((f32[16,6,1,192]{3,2,1,0:T(1,128)}), f32[16,6,1,192]{3,2,1,0:T(1,128)S(1)}, u32[]{:S(2)}, u32[]{:S(2)}) %all-to-all-start.4) | async-done | bytes 73760 | tf_op jit(solution)/shard_map/all_to_all | solution.py:54
  50.7 0.7 reshape.104
  51.5 1.7 fusion
  53.3 0.8 constant_dynamic-slice_fusion
  54.1 10.7 %psum.31 = f32[1,120]{1,0:T(1,128)S(1)} all-reduce(f32[1,120]{1,0:T(1,128)S(1)} %constant_dynamic-slice_fusion), channel_id=1, replica_groups=mesh['rep'=4,'fsdp'=16,'tp'=8] {'rep'}, use_global_device_ids=true, to_apply=%region_3.0 | all-reduce | flops 120 | bytes 960 | tf_op jit(solution)/shard_map/psum | solution.py:79
  65.3 0.6 stack.3
  65.9 5.5 %all-to-all-start.6 = ((f32[16,1,120]{2,1,0:T(1,128)}), f32[16,1,120]{2,1,0:T(1,128)S(1)}, u32[]{:S(2)}, u32[]{:S(2)}) async-start(f32[16,1,120]{2,1,0:T(1,128)} %stack.3), calls=%async_computation.6 | async-start | bytes 16384 | tf_op jit(solution)/shard_map/all_to_all | solution.py:98
  71.8 0.7 reduce.29
  73.1 0.7 reduce.28
  73.9 0.7 reduce.27
  74.6 0.6 reshape.96
  75.5 0.6 mul.73
  77.5 0.8 copy.99
  78.3 24.9 %all-reduce.3.cloned.1.call-done = (f32[24,768]{1,0:T(8,128)}, f32[24,768]{1,0:T(8,128)}, f32[6,3072]{1,0:T(8,128)}) async-done(((f32[24,768]{1,0:T(8,128)}, f32[24,768]{1,0:T(8,128)}, f32[6,3072]{1,0:T(8,128)}), (f32[24,768]{1,0:T(8,128)}, f32[24,768]{1,0:T(8,128)}, f32[6,3072]{1,0:T(8,128)})) %all-reduce.3.cloned.1.call-update) | async-done | bytes 221200 | tf_op jit(solution)/shard_map/psum | solution.py:79
  103.1 1.6 fusion.2
  104.7 1.6 fusion.5
  106.3 1.6 copy.96
  107.9 13.7 %reduce.36 = f32[3072,6]{1,0:T(8,128)S(1)} reduce(f32[3072,1,1,6]{3,2,1,0:T(1,128)S(1)} %bitcast.105, f32[]{:T(128)} %broadcast.98), dimensions={1,2}, to_apply=%bitcast.98.reduce_sub_computation | reduce | bytes 147460
  121.6 1.9 reshape.167
  123.8 1.6 reduce.34
  125.4 0.9 reshape.165
  126.3 9.6 %all-to-all-start.5 = ((f32[16,1,1152]{2,1,0:T(1,128)}), f32[16,1,1152]{2,1,0:T(1,128)S(1)}, u32[]{:S(2)}, u32[]{:S(2)}) async-start(f32[16,1,1152]{2,1,0:T(1,128)} %reshape.167), calls=%async_computation.5 | async-start | bytes 147456 | tf_op jit(solution)/shard_map/all_to_all | solution.py:92
  136.0 0.7 fusion.4
  136.7 0.7 copy.85
  137.4 2.5 %reshape.161 = f32[16,1,1152]{2,1,0:T(1,128)} reshape(f32[768,1,4,6]{3,2,1,0:T(4,128)S(1)} %bitcast.102) | data formatting | bytes 147456
  139.9 4.1 %all-to-all-done.5 = f32[16,1,1152]{2,1,0:T(1,128)S(1)} async-done(((f32[16,1,1152]{2,1,0:T(1,128)}), f32[16,1,1152]{2,1,0:T(1,128)S(1)}, u32[]{:S(2)}, u32[]{:S(2)}) %all-to-all-start.5) | async-done | bytes 73760 | tf_op jit(solution)/shard_map/all_to_all | solution.py:92
  143.9 3.4 %all-to-all-start.3 = ((f32[16,1,1152]{2,1,0:T(1,128)}), f32[16,1,1152]{2,1,0:T(1,128)S(1)}, u32[]{:S(2)}, u32[]{:S(2)}) async-start(f32[16,1,1152]{2,1,0:T(1,128)} %reshape.165), calls=%async_computation.3 | async-start | bytes 147456 | tf_op jit(solution)/shard_map/all_to_all | solution.py:91
  147.4 1.0 multiply_add_fusion
  148.4 7.0 %all-to-all-done.3 = f32[16,1,1152]{2,1,0:T(1,128)S(1)} async-done(((f32[16,1,1152]{2,1,0:T(1,128)}), f32[16,1,1152]{2,1,0:T(1,128)S(1)}, u32[]{:S(2)}, u32[]{:S(2)}) %all-to-all-start.3) | async-done | bytes 73760 | tf_op jit(solution)/shard_map/all_to_all | solution.py:91
  155.4 3.4 %all-to-all-start.1 = ((f32[16,1,1152]{2,1,0:T(1,128)}), f32[16,1,1152]{2,1,0:T(1,128)S(1)}, u32[]{:S(2)}, u32[]{:S(2)}) async-start(f32[16,1,1152]{2,1,0:T(1,128)} %reshape.161), calls=%async_computation.1 | async-start | bytes 147456 | tf_op jit(solution)/shard_map/all_to_all | solution.py:90
  158.8 16.2 %all_gather.3 = f32[251,768]{0,1:T(8,128)} all-gather(f32[251,192]{0,1:T(8,128)S(1)} %get-tuple-element.54), channel_id=1, replica_groups=mesh['rep'=4,'fsdp'=16,'tp'=8] {'rep'}, dimensions={1}, use_global_device_ids=true | all-gather | bytes 963840 | tf_op jit(solution)/shard_map/all_gather | solution.py:114
  175.0 9.3 %all-to-all-start.7 = ((f32[251,16,48]{0,2,1:T(8,128)}), f32[251,16,48]{0,2,1:T(8,128)S(1)}, u32[]{:S(2)}, u32[]{:S(2)}) async-start(f32[251,16,48]{0,2,1:T(8,128)} %bitcast.34), calls=%async_computation.8 | async-start | bytes 1572864 | tf_op jit(solution)/shard_map/all_to_all | solution.py:115
  184.9 0.7 reshape.106
  185.6 0.7 copy.111
  186.3 0.7 copy.110
  187.0 0.7 copy.109
  187.7 0.8 reduce.37
  188.6 2.5 %reshape.168 = f32[3072,1,1,6]{3,2,1,0:T(1,128)S(1)} reshape(f32[16,1152]{1,0:T(8,128)S(1)} %reduce.37) | data formatting | bytes 147456
  191.0 0.6 copy.108
  191.8 0.7 copy.105
  192.5 0.8 reduce.35
  193.3 0.7 reshape.166
  194.3 0.7 copy.104
  195.0 0.8 reduce.33
  195.8 2.0 reshape.162
  197.9 0.8 copy.106
  198.8 0.8 copy.103
  199.7 0.9 reshape.111
  200.6 6.4 %all-to-all-done.7 = f32[251,16,48]{0,2,1:T(8,128)S(1)} async-done(((f32[251,16,48]{0,2,1:T(8,128)}), f32[251,16,48]{0,2,1:T(8,128)S(1)}, u32[]{:S(2)}, u32[]{:S(2)}) %all-to-all-start.7) | async-done | bytes 771104 | tf_op jit(solution)/shard_map/all_to_all | solution.py:115
  207.5 1.3 all_to_all.115
  (77 shorter events, 6.2 us)
Async XLA Ops:
  7.2 44.3 %copy-start = (f32[1,64,768]{2,1,0:T(8,128)S(1)}, f32[1,64,768]{2,1,0:T(8,128)}, u32[]{:S(2)}) copy-start(f32[1,64,768]{2,1,0:T(8,128)} %param.21) | copy-start | bytes 589828
  9.1 18.2 %all-to-all-start.2 = ((f32[16,1,1152]{2,1,0:T(1,128)}), f32[16,1,1152]{2,1,0:T(1,128)S(1)}, u32[]{:S(2)}, u32[]{:S(2)}) async-start(f32[16,1,1152]{2,1,0:T(1,128)} %reshape.163), calls=%async_computation.2 | async-start | bytes 147456 | tf_op jit(solution)/shard_map/all_to_all | solution.py:53
  27.3 11.4 %all-to-all-start = ((f32[16,1,1152]{2,1,0:T(1,128)}), f32[16,1,1152]{2,1,0:T(1,128)S(1)}, u32[]{:S(2)}, u32[]{:S(2)}) async-start(f32[16,1,1152]{2,1,0:T(1,128)} %reshape.159), calls=%async_computation | async-start | bytes 147456 | tf_op jit(solution)/shard_map/all_to_all | solution.py:52
  33.7 17.8 %copy-start.17 = (f32[1,1,251,64]{2,3,1,0:T(8,128)S(1)}, f32[1,1,251,64]{2,3,1,0:T(8,128)}, u32[]{:S(2)}) copy-start(f32[1,1,251,64]{2,3,1,0:T(8,128)} %param.20) | copy-start | bytes 192772
  38.7 11.9 %all-to-all-start.4 = ((f32[16,6,1,192]{3,2,1,0:T(1,128)}), f32[16,6,1,192]{3,2,1,0:T(1,128)S(1)}, u32[]{:S(2)}, u32[]{:S(2)}) async-start(f32[16,6,1,192]{3,2,1,0:T(1,128)} %bitcast.21), calls=%async_computation.4 | async-start | bytes 196608 | tf_op jit(solution)/shard_map/all_to_all | solution.py:54
  42.1 61.0 %all-reduce.3.cloned.1.call-start = ((), (), s32[]{:S(2)}) async-start(), calls=%async_computation.10 | async-start | bytes 491520 | tf_op jit(solution)/shard_map/psum | solution.py:79
  44.0 20.7 %copy-start.18 = (f32[120]{0:T(128)S(1)}, f32[120]{0:T(128)}, u32[]{:S(2)}) copy-start(f32[120]{0:T(128)} %param.30) | copy-start | bytes 1444
  44.0 20.7 %copy-start.19 = (f32[120]{0:T(128)S(1)}, f32[120]{0:T(128)}, u32[]{:S(2)}) copy-start(f32[120]{0:T(128)} %param.25) | copy-start | bytes 1444
  44.0 27.8 %copy-start.10 = (f32[1,18432]{1,0:T(1,128)S(1)}, f32[1,18432]{1,0:T(1,128)}, u32[]{:S(2)}) copy-start(f32[1,18432]{1,0:T(1,128)} %param.24) | copy-start | bytes 221188
  44.1 28.5 %copy-start.14 = (f32[1,18432]{1,0:T(1,128)S(1)}, f32[1,18432]{1,0:T(1,128)}, u32[]{:S(2)}) copy-start(f32[1,18432]{1,0:T(1,128)} %param.29) | copy-start | bytes 221188
  44.1 28.5 %copy-start.15 = (f32[1,18432]{1,0:T(1,128)S(1)}, f32[1,18432]{1,0:T(1,128)}, u32[]{:S(2)}) copy-start(f32[1,18432]{1,0:T(1,128)} %param.28) | copy-start | bytes 221188
  50.6 22.4 %copy-start.11 = (f32[1,18432]{1,0:T(1,128)S(1)}, f32[1,18432]{1,0:T(1,128)}, u32[]{:S(2)}) copy-start(f32[1,18432]{1,0:T(1,128)} %param.23) | copy-start | bytes 221188
  51.4 22.4 %copy-start.12 = (f32[1,18432]{1,0:T(1,128)S(1)}, f32[1,18432]{1,0:T(1,128)}, u32[]{:S(2)}) copy-start(f32[1,18432]{1,0:T(1,128)} %param.22) | copy-start | bytes 221188
  51.4 23.8 %copy-start.13 = (f32[1,18432]{1,0:T(1,128)S(1)}, f32[1,18432]{1,0:T(1,128)}, u32[]{:S(2)}) copy-start(f32[1,18432]{1,0:T(1,128)} %param.27) | copy-start | bytes 221188
  51.4 95.9 %reduce-scatter.2.cloned.1.call-start = ((), (), s32[]{:S(2)}) async-start(), calls=%async_computation.9 | async-start | bytes 983040 | tf_op jit(solution)/shard_map/reduce_scatter | solution.py:110
  53.2 22.9 %copy-start.8 = (f32[1,1,1,48192]{3,2,1,0:T(1,128)S(1)}, f32[1,1,1,48192]{3,2,1,0:T(1,128)}, u32[]{:S(2)}) copy-start(f32[1,1,1,48192]{3,2,1,0:T(1,128)} %param.26) | copy-start | bytes 578308
  65.9 10.9 %copy-start.9 = (f32[1,1,1,48192]{3,2,1,0:T(1,128)S(1)}, f32[1,1,1,48192]{3,2,1,0:T(1,128)}, u32[]{:S(2)}) copy-start(f32[1,1,1,48192]{3,2,1,0:T(1,128)} %param.31) | copy-start | bytes 578308
  65.9 60.5 %all-to-all-start.6 = ((f32[16,1,120]{2,1,0:T(1,128)}), f32[16,1,120]{2,1,0:T(1,128)S(1)}, u32[]{:S(2)}, u32[]{:S(2)}) async-start(f32[16,1,120]{2,1,0:T(1,128)} %stack.3), calls=%async_computation.6 | async-start | bytes 16384 | tf_op jit(solution)/shard_map/all_to_all | solution.py:98
  121.5 2.0 copy-start.3
  121.6 14.4 %copy-start.6 = (f32[24,768]{1,0:T(8,128)S(1)}, f32[24,768]{1,0:T(8,128)}, u32[]{:S(2)}) copy-start(f32[24,768]{1,0:T(8,128)} %reshape.96) | copy-start | bytes 221188
  121.6 14.4 %copy-start.7 = (f32[24,768]{1,0:T(8,128)S(1)}, f32[24,768]{1,0:T(8,128)}, u32[]{:S(2)}) copy-start(f32[24,768]{1,0:T(8,128)} %mul.73) | copy-start | bytes 221188
  121.6 14.4 %copy-start.16 = (f32[24,768]{1,0:T(8,128)S(1)}, f32[24,768]{1,0:T(8,128)}, u32[]{:S(2)}) copy-start(f32[24,768]{1,0:T(8,128)} %get-tuple-element.50) | copy-start | bytes 221188
  126.3 17.6 %all-to-all-start.5 = ((f32[16,1,1152]{2,1,0:T(1,128)}), f32[16,1,1152]{2,1,0:T(1,128)S(1)}, u32[]{:S(2)}, u32[]{:S(2)}) async-start(f32[16,1,1152]{2,1,0:T(1,128)} %reshape.167), calls=%async_computation.5 | async-start | bytes 147456 | tf_op jit(solution)/shard_map/all_to_all | solution.py:92
  136.7 10.7 %copy-start.1 = (f32[251,192]{0,1:T(8,128)S(1)}, f32[251,192]{0,1:T(8,128)}, u32[]{:S(2)}) copy-start(f32[251,192]{0,1:T(8,128)} %copy.99) | copy-start | bytes 578308
  143.9 11.4 %all-to-all-start.3 = ((f32[16,1,1152]{2,1,0:T(1,128)}), f32[16,1,1152]{2,1,0:T(1,128)S(1)}, u32[]{:S(2)}, u32[]{:S(2)}) async-start(f32[16,1,1152]{2,1,0:T(1,128)} %reshape.165), calls=%async_computation.3 | async-start | bytes 147456 | tf_op jit(solution)/shard_map/all_to_all | solution.py:91
  148.4 37.2 %copy-start.2 = (f32[1,1,6,3072]{3,2,1,0:T(8,128)S(1)}, f32[1,1,6,3072]{3,2,1,0:T(8,128)}, u32[]{:S(2)}) copy-start(f32[1,1,6,3072]{3,2,1,0:T(8,128)} %get-tuple-element.55) | copy-start | bytes 221188
  148.4 37.9 %copy-start.4 = (f32[1,1,24,768]{3,2,1,0:T(8,128)S(1)}, f32[1,1,24,768]{3,2,1,0:T(8,128)}, u32[]{:S(2)}) copy-start(f32[1,1,24,768]{3,2,1,0:T(8,128)} %get-tuple-element.57) | copy-start | bytes 221188
  148.4 38.6 %copy-start.5 = (f32[1,1,24,768]{3,2,1,0:T(8,128)S(1)}, f32[1,1,24,768]{3,2,1,0:T(8,128)}, u32[]{:S(2)}) copy-start(f32[1,1,24,768]{3,2,1,0:T(8,128)} %get-tuple-element.59) | copy-start | bytes 221188
  155.4 19.7 %all-to-all-start.1 = ((f32[16,1,1152]{2,1,0:T(1,128)}), f32[16,1,1152]{2,1,0:T(1,128)S(1)}, u32[]{:S(2)}, u32[]{:S(2)}) async-start(f32[16,1,1152]{2,1,0:T(1,128)} %reshape.161), calls=%async_computation.1 | async-start | bytes 147456 | tf_op jit(solution)/shard_map/all_to_all | solution.py:90
  175.0 32.0 %all-to-all-start.7 = ((f32[251,16,48]{0,2,1:T(8,128)}), f32[251,16,48]{0,2,1:T(8,128)S(1)}, u32[]{:S(2)}, u32[]{:S(2)}) async-start(f32[251,16,48]{0,2,1:T(8,128)} %bitcast.34), calls=%async_computation.8 | async-start | bytes 1572864 | tf_op jit(solution)/shard_map/all_to_all | solution.py:115
Sparse Core Ops, SparseCore 0:
  51.5 51.5 all-reduce.2
  106.8 31.1 reduce-scatter.1
